TPU v7x, 32 devices: a whole 2x2x4 slice. The times are simulated.
32 devices in a mesh: grp: 2 (over y), blk: 4 (over z), walk: 2 (over x), sub: 2 (over core).
Axes of the slice: x: 2, y: 2, z: 4, core: 2. Of those that a mesh axis runs over, the one named last changes fastest.
Arguments:
- walker_mats: bfloat16 [8, 2048, 2048], P(('grp', 'blk'), 'walk'), parts along dimension 0, may hold values from -0.0029296875 to 0.0029296875
- vertex: int32 [8, 2048], P(('grp', 'blk')), parts along dimension 0, may hold values from 0 to 8191
- weights: float32 [8], P('grp'), parts along dimension 0, may hold values from 0.5 to 1.5
- transfer_table: int32 [16, 2560], replicated, may hold values from 0 to 2559, each once within a row
- g4_old: float32 [32, 16, 2560], P(('grp', 'blk', 'walk', 'sub')), parts along dimension 0, may hold values from -2 to 2
Outputs:
- g4_new: float32 [32, 16, 2560], P(('grp', 'blk', 'walk', 'sub')), parts along dimension 0
There are 2 independent parts, one for each index of `grp`. A program takes and returns all parts, laid end to end along the dimension named above; an argument that names none is the same for every part. Nothing has to cross between parts.
All inputs are finite; a program needn't handle non-finite values.
Results may differ from a plain program's by a relative error of at most 0.0041.
Values may be sent and summed in bfloat16 or wider, within the bound.
A program may use at most 64 MiB of HBM per device.

v0:
```python
import functools
import math

import jax
import jax.numpy as jnp
import numpy as np
from jax import lax
from jax.experimental import pallas as pl
from jax.experimental.pallas import tpu as pltpu
from jax.sharding import PartitionSpec as P

TQ = 4
RSTEPS = 4

phase_period = 8192
quarter = phase_period // 4
lanes = 128
fine_count = 64
column_block = 256


def cos_sin(residue):
    turns = (residue + quarter // 2) >> 11
    x = (residue - (turns << 11)).astype(jnp.float32) * (2.0 * math.pi / phase_period)
    y = x * x
    s = x + x * y * (-1 / 6 + y * (1 / 120 + y * (-1 / 5040 + y * (1 / 362880))))
    c = 1.0 + y * (-0.5 + y * (1 / 24 + y * (-1 / 720 + y * (1 / 40320 + y * (-1 / 3628800)))))
    odd = (turns & 1) == 1
    cos = jnp.where(odd, s, c)
    sin = jnp.where(odd, c, s)
    cos = jnp.where(((turns + 1) & 2) == 2, -cos, cos)
    sin = jnp.where((turns & 2) == 2, -sin, sin)
    return cos, sin


def green_kernel(
    mats, vertex, window, gathered,
    slab, fine_plus, fine_minus, coarse_cos, coarse_sin, pair, partial, landed, mine,
    slab_sem, send_one, recv_one, send_two, recv_two,
):
    blk_count, walk_count, sub_count = (lax.axis_size(a) for a in ("blk", "walk", "sub"))
    b, w, s = (lax.axis_index(a) for a in ("blk", "walk", "sub"))
    near = walk_count * sub_count
    place = w * sub_count + s
    depth = slab.shape[1]
    own_rows = slab.shape[0]
    start = pl.multiple_of(s * depth, lanes)
    fetch = pltpu.make_async_copy(mats.at[0, :, pl.ds(start, depth)], slab, slab_sem)
    fetch.start()

    def near_id(distance):
        peer = lax.rem(place + distance, near)
        return {"walk": peer // sub_count, "sub": lax.rem(peer, sub_count)}

    def far_id(distance):
        return {"blk": lax.rem(b + distance, blk_count)}

    barrier = pltpu.get_barrier_semaphore()
    for d in range(1, near):
        pl.semaphore_signal(barrier, inc=1, device_id=near_id(d), device_id_type=pl.DeviceIdType.MESH)
    for d in range(1, blk_count):
        pl.semaphore_signal(barrier, inc=1, device_id=far_id(d), device_id_type=pl.DeviceIdType.MESH)

    verts = vertex[:, pl.ds(start, depth)]
    fine = lax.broadcasted_iota(jnp.int32, (fine_count, depth), 0)
    cos, sin = cos_sin((fine * verts) & (phase_period - 1))
    fine_plus[...] = cos + sin
    fine_minus[...] = cos - sin
    coarse = lax.broadcasted_iota(jnp.int32, coarse_cos.shape, 0) * fine_count
    cos, sin = cos_sin((coarse * verts) & (phase_period - 1))
    coarse_cos[...] = cos
    coarse_sin[...] = sin
    own = vertex[:, pl.ds(pl.multiple_of(w * own_rows, lanes), own_rows)]
    cos, sin = cos_sin((window[...] * own) & (phase_period - 1))
    left = (cos + sin).astype(jnp.bfloat16)

    fetch.wait()
    inner = jnp.dot(left, slab[...], preferred_element_type=jnp.float32)
    rows = inner.shape[0]
    high = inner.astype(jnp.bfloat16)
    pair[0:rows, :] = high
    pair[rows:2 * rows, :] = (inner - high.astype(jnp.float32)).astype(jnp.bfloat16)

    per_block = column_block // fine_count
    share = rows // near

    @pl.loop(0, partial.shape[2] // column_block)
    def _(block):
        pieces = []
        for part in range(per_block):
            row = block * per_block + part
            c = coarse_cos[pl.ds(row, 1), :]
            t = coarse_sin[pl.ds(row, 1), :]
            pieces.append((c * fine_plus[...] + t * fine_minus[...]).astype(jnp.bfloat16))
        table = jnp.concatenate(pieces, axis=0)
        both = lax.dot_general(
            pair[...], table, (((1,), (1,)), ((), ())), preferred_element_type=jnp.float32
        )
        total = both[0:rows] + both[rows:2 * rows]
        columns = pl.ds(pl.multiple_of(block * column_block, column_block), column_block)
        for q in range(near):
            partial[q, :, columns] = total[q * share:(q + 1) * share]

    pl.semaphore_wait(barrier, near - 1 + blk_count - 1)
    first = []
    for d in range(1, near):
        copy = pltpu.make_async_remote_copy(
            src_ref=partial.at[lax.rem(place + d, near)],
            dst_ref=landed.at[d - 1],
            send_sem=send_one.at[d - 1],
            recv_sem=recv_one.at[d - 1],
            device_id=near_id(d),
            device_id_type=pl.DeviceIdType.MESH,
        )
        copy.start()
        first.append(copy)
    total = partial[place]
    for d in range(1, near):
        first[d - 1].wait_recv()
        total = total + landed[d - 1]
    mine[...] = total.astype(jnp.bfloat16)
    gathered[b] = total.astype(jnp.bfloat16)
    second = []
    for d in range(1, blk_count):
        copy = pltpu.make_async_remote_copy(
            src_ref=mine,
            dst_ref=gathered.at[b],
            send_sem=send_two.at[d - 1],
            recv_sem=recv_two.at[d - 1],
            device_id=far_id(d),
            device_id_type=pl.DeviceIdType.MESH,
        )
        copy.start()
        second.append(copy)
    for copy in first:
        copy.wait_send()
    for copy in second:
        copy.wait()


def panel_kernel(weights, gathered, table, old, new, wide, source, scaled):
    walkers, rows, columns = gathered.shape
    blk_count = lax.axis_size("blk")
    rows_own = rows // blk_count
    b = lax.axis_index("blk")
    transfers = table.shape[0]
    sublanes = 8
    blocks = columns // lanes
    for n in range(walkers):
        wide[n] = gathered[n].astype(jnp.float32)
    for inner in range(rows_own):
        for n in range(walkers):
            for step in range(RSTEPS):
                row = lax.rem(b + RSTEPS * blk_count - step, blk_count) * rows_own + inner
                line = wide[n, pl.ds(row, 1), :]
                source[n, step * TQ:(step + 1) * TQ, :] = jnp.broadcast_to(line, (TQ, columns))
                if step == 0:
                    scaled[n, :, :] = jnp.broadcast_to(line * (weights[n] / walkers), (sublanes, columns))

        @pl.loop(0, blocks)
        def _(block):
            here = pl.ds(pl.multiple_of(block * lanes, lanes), lanes)
            for half in range(transfers // sublanes):
                span = slice(half * sublanes, (half + 1) * sublanes)
                index = table[span, here]
                low = index & (lanes - 1)
                which = index >> 7
                picked = [jnp.zeros((sublanes, lanes), jnp.float32) for _ in range(walkers)]
                for k in range(blocks):
                    hit = which == k
                    for n in range(walkers):
                        found = jnp.take_along_axis(
                            source[n, span, k * lanes:(k + 1) * lanes], low, axis=1,
                            mode="promise_in_bounds",
                        )
                        picked[n] = jnp.where(hit, found, picked[n])
                total = picked[0] * scaled[0, :, here]
                for n in range(1, walkers):
                    total = total + picked[n] * scaled[n, :, here]
                new[inner, span, here] = old[inner, span, here] + total


def local(walker_mats, vertex, weights, transfer_table, g4_old):
    blk_count, walk_count, sub_count = (lax.axis_size(a) for a in ("blk", "walk", "sub"))
    near = walk_count * sub_count
    rows_own, transfers, columns = g4_old.shape
    own_rows, vertices = walker_mats.shape[1:]
    depth = vertices // sub_count
    share = blk_count * rows_own
    rows = near * share
    p = np.arange(rows)
    inner, blk_part, near_part = p % rows_own, p // rows_own % blk_count, p // share
    window = jnp.asarray(((blk_part * near + near_part) * rows_own + inner)[:, None], jnp.int32)
    vmem = pl.BlockSpec(memory_space=pltpu.VMEM)
    gathered = pl.pallas_call(
        green_kernel,
        out_shape=jax.ShapeDtypeStruct((blk_count, share, columns), jnp.bfloat16),
        in_specs=[pl.BlockSpec(memory_space=pl.ANY), vmem, vmem],
        out_specs=vmem,
        scratch_shapes=[
            pltpu.VMEM((own_rows, depth), jnp.bfloat16),
            pltpu.VMEM((fine_count, depth), jnp.float32),
            pltpu.VMEM((fine_count, depth), jnp.float32),
            pltpu.VMEM((columns // fine_count, depth), jnp.float32),
            pltpu.VMEM((columns // fine_count, depth), jnp.float32),
            pltpu.VMEM((2 * rows, depth), jnp.bfloat16),
            pltpu.VMEM((near, share, columns), jnp.float32),
            pltpu.VMEM((near - 1, share, columns), jnp.float32),
            pltpu.VMEM((share, columns), jnp.bfloat16),
            pltpu.SemaphoreType.DMA,
            pltpu.SemaphoreType.DMA((near - 1,)),
            pltpu.SemaphoreType.DMA((near - 1,)),
            pltpu.SemaphoreType.DMA((blk_count - 1,)),
            pltpu.SemaphoreType.DMA((blk_count - 1,)),
        ],
        compiler_params=pltpu.CompilerParams(collective_id=0, has_side_effects=True),
        name="green",
    )(walker_mats, vertex, window)
    return pl.pallas_call(
        panel_kernel,
        out_shape=jax.ShapeDtypeStruct(g4_old.shape, jnp.float32),
        in_specs=[pl.BlockSpec(memory_space=pltpu.SMEM), vmem, vmem, vmem],
        out_specs=vmem,
        scratch_shapes=[
            pltpu.VMEM((blk_count, share, columns), jnp.float32),
            pltpu.VMEM((blk_count, transfers, columns), jnp.float32),
            pltpu.VMEM((blk_count, 8, columns), jnp.float32),
        ],
        name="panels",
    )(weights, gathered, transfer_table, g4_old)


def solution(mesh):
    in_specs = (
        P(("grp", "blk"), "walk", None),
        P(("grp", "blk"), None),
        P("grp"),
        P(),
        P(("grp", "blk", "walk", "sub"), None, None),
    )
    out_specs = P(("grp", "blk", "walk", "sub"), None, None)
    return jax.shard_map(local, mesh=mesh, in_specs=in_specs, out_specs=out_specs, check_vma=False)
```

profile of v0, /device:TPU:0, one launch (start us, length us, event | category | flops | bytes accessed | tf_op | source)
XLA Modules:
  0.0 23.6 jit_solution(17636127544554765934)
XLA Ops:
  0.0 16.7 %green.1.gathered = bf16[4,4,2560]{2,1,0:T(4,128)(2,1)} custom-call(bf16[1,1024,2048]{2,1,0:T(8,128)(2,1)} %mats.1, s32[1,2048]{1,0:T(1,128)} %vertex.1, s32[16,1]{1,0:T(8,128)} %constant.2.clone.window), custom_call_target="tpu_custom_call" | custom-call | tf_op jit(solution)/shard_map/green/pallas_call | solution.py:195
  16.7 6.9 %panels.1 = f32[1,16,2560]{2,1,0:T(8,128)} custom-call(f32[4]{0:T(128)} %weights.1, bf16[4,4,2560]{2,1,0:T(4,128)(2,1)} %green.1.gathered, s32[16,2560]{1,0:T(8,128)} %table.1, f32[1,16,2560]{2,1,0:T(8,128)} %old.1), custom_call_target="tpu_custom_call" | custom-call | tf_op jit(solution)/shard_map/panels/pallas_call | solution.py:219
where the time goes:
time: 23.8 us; the launch traced here: 23.6 us
  Pallas kernels  23.6 us (99%)
    pallas_call x1, Pallas kernels, local(): pl.pallas_call(green_kernel, out_shape=jax.ShapeDtypeStruct((blk_count, s...  16.7 us
    pallas_call x1, Pallas kernels, local(): pl.pallas_call(panel_kernel, out_shape=jax.ShapeDtypeStruct(g4_old.shape,...  6.85 us

commit v1 on v0

v1 whole, which is shorter than its diff:
```python
import math

import jax
import jax.numpy as jnp
import numpy as np
from jax import lax
from jax.experimental import pallas as pl
from jax.experimental.pallas import tpu as pltpu
from jax.sharding import PartitionSpec as P

TQ = 4
RSTEPS = 4

half_period = 16384
lanes = 128
sublanes = 8
column_block = 256
chunk_blocks = 2
group_blocks = 4


def cos_sin(residue):
    turns = (residue + half_period // 8) >> 12
    x = (residue - (turns << 12)).astype(jnp.float32) * (2.0 * math.pi / half_period)
    y = x * x
    s = x + x * y * (-1 / 6 + y * (1 / 120 + y * (-1 / 5040 + y * (1 / 362880))))
    c = 1.0 + y * (-0.5 + y * (1 / 24 + y * (-1 / 720 + y * (1 / 40320 + y * (-1 / 3628800)))))
    odd = (turns & 1) == 1
    cos = jnp.where(odd, s, c)
    sin = jnp.where(odd, c, s)
    cos = jnp.where(((turns + 1) & 2) == 2, -cos, cos)
    sin = jnp.where((turns & 2) == 2, -sin, sin)
    return cos, sin


def kernel(
    weights, mats, vertex, window, table, delta,
    slab, low, which, turn_cos, turn_sin, fine_cos, fine_sin, coarse_plus, coarse_minus, pair,
    partial, landed, gathered, wide, source, scaled,
    slab_sem, send_one, recv_one, send_two, recv_two,
):
    blk_count, walk_count, sub_count = (lax.axis_size(a) for a in ("blk", "walk", "sub"))
    b, w, s = (lax.axis_index(a) for a in ("blk", "walk", "sub"))
    near = walk_count * sub_count
    place = w * sub_count + s
    own_rows, depth = slab.shape
    rows = window.shape[0]
    share = rows // near
    columns = partial.shape[2]
    transfers = table.shape[0]
    rows_own = share // blk_count
    chunk = chunk_blocks * column_block
    chunks = columns // chunk
    start = pl.multiple_of(s * depth, lanes)
    fetch = pltpu.make_async_copy(mats.at[0, :, pl.ds(start, depth)], slab, slab_sem)
    fetch.start()

    def near_id(distance):
        peer = lax.rem(place + distance, near)
        return {"walk": peer // sub_count, "sub": lax.rem(peer, sub_count)}

    def far_id(distance):
        return {"blk": lax.rem(b + distance, blk_count)}

    def span_of(c):
        return pl.ds(pl.multiple_of(c * chunk, chunk), chunk)

    def near_copy(c, d):
        return pltpu.make_async_remote_copy(
            src_ref=partial.at[lax.rem(place + d, near), :, span_of(c)],
            dst_ref=landed.at[d - 1, :, span_of(c)],
            send_sem=send_one.at[c, d - 1],
            recv_sem=recv_one.at[c, d - 1],
            device_id=near_id(d),
            device_id_type=pl.DeviceIdType.MESH,
        )

    def far_copy(c, d):
        return pltpu.make_async_remote_copy(
            src_ref=gathered.at[0, :, span_of(c)],
            dst_ref=gathered.at[d, :, span_of(c)],
            send_sem=send_two.at[c, d - 1],
            recv_sem=recv_two.at[c, d - 1],
            device_id=far_id(d),
            device_id_type=pl.DeviceIdType.MESH,
        )

    barrier = pltpu.get_barrier_semaphore()
    for d in range(1, near):
        pl.semaphore_signal(barrier, inc=1, device_id=near_id(d), device_id_type=pl.DeviceIdType.MESH)
    for d in range(1, blk_count):
        pl.semaphore_signal(barrier, inc=1, device_id=far_id(d), device_id_type=pl.DeviceIdType.MESH)

    def row_of(count):
        return lax.broadcasted_iota(jnp.int32, (count, depth), 0)

    def phases(factor, verts):
        return cos_sin((factor * verts) & (half_period - 1))

    verts = vertex[:, pl.ds(start, depth)]
    own = vertex[:, pl.ds(pl.multiple_of(w * own_rows, lanes), own_rows)]
    cos, sin = phases(window[...] * 2, own)
    left = (cos + sin).astype(jnp.bfloat16)
    cos, sin = phases(row_of(coarse_plus.shape[0]) * (2 * column_block) + (column_block - 1), verts)
    coarse_plus[...] = cos + sin
    coarse_minus[...] = cos - sin
    steps = turn_cos.shape[0]
    cos, sin = phases(row_of(steps) * (2 * sublanes), verts)
    turn_cos[...] = cos
    turn_sin[...] = sin
    cos, sin = phases(row_of(sublanes) * 2 + 1, verts)
    for h in range(steps):
        ch, sh = turn_cos[h:h + 1, :], turn_sin[h:h + 1, :]
        fine_cos[h * sublanes:(h + 1) * sublanes, :] = ch * cos - sh * sin
        fine_sin[h * sublanes:(h + 1) * sublanes, :] = sh * cos + ch * sin

    fetch.wait()
    inner = jnp.dot(left, slab[...], preferred_element_type=jnp.float32)
    high = inner.astype(jnp.bfloat16)
    pair[0:rows, :] = high
    pair[rows:2 * rows, :] = (inner - high.astype(jnp.float32)).astype(jnp.bfloat16)

    pl.semaphore_wait(barrier, near - 1 + blk_count - 1)

    @pl.loop(0, chunks)
    def _(c):
        for part in range(chunk_blocks):
            block = c * chunk_blocks + part
            a_plus = coarse_plus[pl.ds(block, 1), :]
            a_minus = coarse_minus[pl.ds(block, 1), :]
            below, above = [], []
            for g in range(lanes // 16):
                p = a_plus * fine_cos[g * 16:(g + 1) * 16, :]
                q = a_minus * fine_sin[g * 16:(g + 1) * 16, :]
                below.append((p - q).astype(jnp.bfloat16))
                above.append((p + q).astype(jnp.bfloat16))
            both = lax.dot_general(
                pair[...], jnp.concatenate(below + above, axis=0), (((1,), (1,)), ((), ())),
                preferred_element_type=jnp.float32,
            )
            total = both[0:rows] + both[rows:2 * rows]
            here = pl.ds(pl.multiple_of(block * column_block, column_block), column_block)
            for q in range(near):
                partial[q, :, here] = total[q * share:(q + 1) * share]
        for d in range(1, near):
            near_copy(c, d).start()

    index = table[...]
    which[...] = index >> 7
    low[...] = (index & (lanes - 1)) ^ jnp.where((index & lanes) == 0, lanes - 1, 0)
    delta[...] = jnp.zeros_like(delta)

    @pl.loop(0, chunks)
    def _(c):
        here = span_of(c)
        total = partial[place, :, here]
        for d in range(1, near):
            near_copy(c, d).wait_recv()
            total = total + landed[d - 1, :, here]
        gathered[0, :, here] = total.astype(jnp.bfloat16)
        for d in range(1, blk_count):
            far_copy(c, d).start()

    back = lanes - 1 - lax.broadcasted_iota(jnp.int32, (sublanes, lanes), 1)

    def walker(d):
        wide[...] = gathered[d].astype(jnp.float32)
        weight = weights[lax.rem(b + blk_count - d, blk_count)] / weights.shape[0]
        for r in range(rows_own):
            for step in range(RSTEPS):
                row = lax.rem(b + RSTEPS * blk_count - step, blk_count) * rows_own + r
                line = wide[pl.ds(row, 1), :]
                source[step * TQ:(step + 1) * TQ, :] = jnp.broadcast_to(line, (TQ, columns))
                if step == 0:
                    tall = jnp.broadcast_to(line * weight, (sublanes, columns))
                    for k in range(columns // lanes):
                        piece = tall[:, k * lanes:(k + 1) * lanes]
                        if k % 2 == 0:
                            piece = jnp.take_along_axis(piece, back, axis=1, mode="promise_in_bounds")
                        scaled[:, k * lanes:(k + 1) * lanes] = piece

            @pl.loop(0, columns // (lanes * group_blocks))
            def _(group):
                for half in range(transfers // sublanes):
                    span = slice(half * sublanes, (half + 1) * sublanes)
                    heres = [
                        pl.ds(pl.multiple_of((group * group_blocks + i) * lanes, lanes), lanes)
                        for i in range(group_blocks)
                    ]
                    lows = [low[span, here] for here in heres]
                    blocks = [which[span, here] for here in heres]
                    picked = [jnp.zeros((sublanes, lanes), jnp.float32) for _ in heres]
                    for k in range(columns // lanes):
                        held = source[span, k * lanes:(k + 1) * lanes]
                        for i in range(group_blocks):
                            found = jnp.take_along_axis(held, lows[i], axis=1, mode="promise_in_bounds")
                            picked[i] = jnp.where(blocks[i] == k, found, picked[i])
                    for i, here in enumerate(heres):
                        delta[r, span, here] += picked[i] * scaled[:, here]

    walker(0)

    @pl.loop(1, blk_count)
    def _(d):
        for c in range(chunks):
            far_copy(c, d).wait_recv()
        walker(d)

    @pl.loop(0, chunks)
    def _(c):
        for d in range(1, near):
            near_copy(c, d).wait_send()
        for d in range(1, blk_count):
            far_copy(c, d).wait_send()


def local(walker_mats, vertex, weights, transfer_table, g4_old):
    blk_count, walk_count, sub_count = (lax.axis_size(a) for a in ("blk", "walk", "sub"))
    near = walk_count * sub_count
    rows_own, transfers, columns = g4_old.shape
    own_rows, vertices = walker_mats.shape[1:]
    depth = vertices // sub_count
    share = blk_count * rows_own
    rows = near * share
    chunks = columns // (column_block * chunk_blocks)
    coarse = -(-(columns // column_block) // sublanes) * sublanes
    p = np.arange(rows)
    inner, blk_part, near_part = p % rows_own, p // rows_own % blk_count, p // share
    window = jnp.asarray(((blk_part * near + near_part) * rows_own + inner)[:, None], jnp.int32)
    vmem = pl.BlockSpec(memory_space=pltpu.VMEM)
    delta = pl.pallas_call(
        kernel,
        out_shape=jax.ShapeDtypeStruct(g4_old.shape, jnp.float32),
        in_specs=[pl.BlockSpec(memory_space=pltpu.SMEM), pl.BlockSpec(memory_space=pl.ANY), vmem, vmem, vmem],
        out_specs=vmem,
        scratch_shapes=[
            pltpu.VMEM((own_rows, depth), jnp.bfloat16),
            pltpu.VMEM((transfers, columns), jnp.int32),
            pltpu.VMEM((transfers, columns), jnp.int32),
            pltpu.VMEM((lanes // sublanes, depth), jnp.float32),
            pltpu.VMEM((lanes // sublanes, depth), jnp.float32),
            pltpu.VMEM((lanes, depth), jnp.float32),
            pltpu.VMEM((lanes, depth), jnp.float32),
            pltpu.VMEM((coarse, depth), jnp.float32),
            pltpu.VMEM((coarse, depth), jnp.float32),
            pltpu.VMEM((2 * rows, depth), jnp.bfloat16),
            pltpu.VMEM((near, share, columns), jnp.float32),
            pltpu.VMEM((near - 1, share, columns), jnp.float32),
            pltpu.VMEM((blk_count, share, columns), jnp.bfloat16),
            pltpu.VMEM((share, columns), jnp.float32),
            pltpu.VMEM((transfers, columns), jnp.float32),
            pltpu.VMEM((sublanes, columns), jnp.float32),
            pltpu.SemaphoreType.DMA,
            pltpu.SemaphoreType.DMA((chunks, near - 1)),
            pltpu.SemaphoreType.DMA((chunks, near - 1)),
            pltpu.SemaphoreType.DMA((chunks, blk_count - 1)),
            pltpu.SemaphoreType.DMA((chunks, blk_count - 1)),
        ],
        compiler_params=pltpu.CompilerParams(collective_id=0, has_side_effects=True),
        name="panels",
    )(weights, walker_mats, vertex, window, transfer_table)
    return g4_old + delta


def solution(mesh):
    in_specs = (
        P(("grp", "blk"), "walk", None),
        P(("grp", "blk"), None),
        P("grp"),
        P(),
        P(("grp", "blk", "walk", "sub"), None, None),
    )
    out_specs = P(("grp", "blk", "walk", "sub"), None, None)
    return jax.shard_map(local, mesh=mesh, in_specs=in_specs, out_specs=out_specs, check_vma=False)
```

time: 23.8 us -> 25.7 us (1.080)
  other arithmetic: 0 us -> 1.6 us
  Pallas kernels: 23.6 us -> 23.9 us
    add x0 -> x1, other arithmetic: none -> 1.6 us  [local(): return g4_old + delta]
    pallas_call x2 -> x1, Pallas kernels: 23.6 us -> 23.9 us  [local(): pl.pallas_call(kernel, out_shape=jax.ShapeDtypeStruct(g4_old.shape, jnp.f...]
where the time goes in v1:
time: 25.7 us; the launch traced here: 25.5 us
  Pallas kernels  23.9 us (93%)
  other arithmetic  1.6 us (6%)
    pallas_call x1, Pallas kernels, local(): pl.pallas_call(kernel, out_shape=jax.ShapeDtypeStruct(g4_old.shape, jnp.f...  23.9 us
    add x1, other arithmetic, local(): return g4_old + delta  1.6 us

profile of v1, /device:TPU:0, one launch (start us, length us, event | category | flops | bytes accessed | tf_op | source)
XLA Modules:
  0.0 25.5 jit_solution(17204503593556437942)
XLA Ops:
  0.0 0.0 copy-start
  0.0 23.9 %panels.1 = f32[1,16,2560]{2,1,0:T(8,128)} custom-call(f32[4]{0:T(128)} %weights.1, bf16[1,1024,2048]{2,1,0:T(8,128)(2,1)} %mats.1, s32[1,2048]{1,0:T(1,128)} %vertex.1, s32[16,1]{1,0:T(8,128)} %constant.2.clone.window, s32[16,2560]{1,0:T(8,128)} %table.1), custom_call_target="tpu_custom_call" | custom-call | tf_op jit(solution)/shard_map/panels/pallas_call | solution.py:231
  23.9 0.0 copy-done
  23.9 1.6 %add.3 = f32[1,16,2560]{2,1,0:T(8,128)} add(f32[1,16,2560]{2,1,0:T(8,128)S(1)} %copy-done, f32[1,16,2560]{2,1,0:T(8,128)} %panels.1) | non-fusion elementwise | flops 40960 | bytes 491520 | tf_op jit(solution)/shard_map/add | solution.py:262
Async XLA Ops:
  0.0 23.9 %copy-start = (f32[1,16,2560]{2,1,0:T(8,128)S(1)}, f32[1,16,2560]{2,1,0:T(8,128)}, u32[]{:S(2)}) copy-start(f32[1,16,2560]{2,1,0:T(8,128)} %param.10) | copy-start | bytes 491524

commit v2 on v1

--- a/solution.py
+++ b/solution.py
@@ -16,7 +16,6 @@
 sublanes = 8
 column_block = 256
 chunk_blocks = 2
-group_blocks = 4
 
 
 def cos_sin(residue):
@@ -34,10 +33,10 @@
 
 
 def kernel(
-    weights, mats, vertex, window, table, delta,
-    slab, low, which, turn_cos, turn_sin, fine_cos, fine_sin, coarse_plus, coarse_minus, pair,
+    weights, mats, vertex, window, table, old, panels,
+    slab, base, low, which, turn_cos, turn_sin, fine_cos, fine_sin, coarse_plus, coarse_minus, pair,
     partial, landed, gathered, wide, source, scaled,
-    slab_sem, send_one, recv_one, send_two, recv_two,
+    slab_sem, table_sem, base_sem, send_one, recv_one, send_two, recv_two,
 ):
     blk_count, walk_count, sub_count = (lax.axis_size(a) for a in ("blk", "walk", "sub"))
     b, w, s = (lax.axis_index(a) for a in ("blk", "walk", "sub"))
@@ -47,13 +46,17 @@
     rows = window.shape[0]
     share = rows // near
     columns = partial.shape[2]
-    transfers = table.shape[0]
+    transfers = low.shape[0]
     rows_own = share // blk_count
     chunk = chunk_blocks * column_block
     chunks = columns // chunk
     start = pl.multiple_of(s * depth, lanes)
     fetch = pltpu.make_async_copy(mats.at[0, :, pl.ds(start, depth)], slab, slab_sem)
     fetch.start()
+    fetch_table = pltpu.make_async_copy(table, low, table_sem)
+    fetch_table.start()
+    fetch_base = pltpu.make_async_copy(old, base, base_sem)
+    fetch_base.start()
 
     def near_id(distance):
         peer = lax.rem(place + distance, near)
@@ -109,6 +112,7 @@
     turn_cos[...] = cos
     turn_sin[...] = sin
     cos, sin = phases(row_of(sublanes) * 2 + 1, verts)
+
     for h in range(steps):
         ch, sh = turn_cos[h:h + 1, :], turn_sin[h:h + 1, :]
         fine_cos[h * sublanes:(h + 1) * sublanes, :] = ch * cos - sh * sin
@@ -124,7 +128,8 @@
 
     @pl.loop(0, chunks)
     def _(c):
-        for part in range(chunk_blocks):
+        @pl.loop(0, chunk_blocks)
+        def _(part):
             block = c * chunk_blocks + part
             a_plus = coarse_plus[pl.ds(block, 1), :]
             a_minus = coarse_minus[pl.ds(block, 1), :]
@@ -142,13 +147,16 @@
             here = pl.ds(pl.multiple_of(block * column_block, column_block), column_block)
             for q in range(near):
                 partial[q, :, here] = total[q * share:(q + 1) * share]
+
         for d in range(1, near):
             near_copy(c, d).start()
 
-    index = table[...]
+    fetch_table.wait()
+    index = low[...]
     which[...] = index >> 7
     low[...] = (index & (lanes - 1)) ^ jnp.where((index & lanes) == 0, lanes - 1, 0)
-    delta[...] = jnp.zeros_like(delta)
+    fetch_base.wait()
+    panels[...] = base[...]
 
     @pl.loop(0, chunks)
     def _(c):
@@ -163,48 +171,55 @@
 
     back = lanes - 1 - lax.broadcasted_iota(jnp.int32, (sublanes, lanes), 1)
 
-    def walker(d):
-        wide[...] = gathered[d].astype(jnp.float32)
-        weight = weights[lax.rem(b + blk_count - d, blk_count)] / weights.shape[0]
+    def walkers(first, count, group_blocks):
         for r in range(rows_own):
-            for step in range(RSTEPS):
-                row = lax.rem(b + RSTEPS * blk_count - step, blk_count) * rows_own + r
-                line = wide[pl.ds(row, 1), :]
-                source[step * TQ:(step + 1) * TQ, :] = jnp.broadcast_to(line, (TQ, columns))
-                if step == 0:
-                    tall = jnp.broadcast_to(line * weight, (sublanes, columns))
-                    for k in range(columns // lanes):
-                        piece = tall[:, k * lanes:(k + 1) * lanes]
-                        if k % 2 == 0:
-                            piece = jnp.take_along_axis(piece, back, axis=1, mode="promise_in_bounds")
-                        scaled[:, k * lanes:(k + 1) * lanes] = piece
+            for n in range(count):
+                wide[...] = gathered[first + n].astype(jnp.float32)
+                weight = weights[lax.rem(b + blk_count - first - n, blk_count)] / weights.shape[0]
+                for step in range(RSTEPS):
+                    row = lax.rem(b + RSTEPS * blk_count - step, blk_count) * rows_own + r
+                    line = wide[pl.ds(row, 1), :]
+                    source[n, step * TQ:(step + 1) * TQ, :] = jnp.broadcast_to(line, (TQ, columns))
+                    if step == 0:
+                        tall = jnp.broadcast_to(line * weight, (sublanes, columns))
+                        for k in range(columns // lanes):
+                            piece = tall[:, k * lanes:(k + 1) * lanes]
+                            if k % 2 == 0:
+                                piece = jnp.take_along_axis(piece, back, axis=1, mode="promise_in_bounds")
+                            scaled[n, :, k * lanes:(k + 1) * lanes] = piece
 
             @pl.loop(0, columns // (lanes * group_blocks))
             def _(group):
-                for half in range(transfers // sublanes):
-                    span = slice(half * sublanes, (half + 1) * sublanes)
-                    heres = [
-                        pl.ds(pl.multiple_of((group * group_blocks + i) * lanes, lanes), lanes)
-                        for i in range(group_blocks)
-                    ]
-                    lows = [low[span, here] for here in heres]
-                    blocks = [which[span, here] for here in heres]
-                    picked = [jnp.zeros((sublanes, lanes), jnp.float32) for _ in heres]
-                    for k in range(columns // lanes):
-                        held = source[span, k * lanes:(k + 1) * lanes]
-                        for i in range(group_blocks):
-                            found = jnp.take_along_axis(held, lows[i], axis=1, mode="promise_in_bounds")
-                            picked[i] = jnp.where(blocks[i] == k, found, picked[i])
-                    for i, here in enumerate(heres):
-                        delta[r, span, here] += picked[i] * scaled[:, here]
-
-    walker(0)
-
-    @pl.loop(1, blk_count)
-    def _(d):
-        for c in range(chunks):
-            far_copy(c, d).wait_recv()
-        walker(d)
+                for i in range(group_blocks):
+                    here = pl.ds(pl.multiple_of((group * group_blocks + i) * lanes, lanes), lanes)
+                    for half in range(transfers // sublanes):
+                        span = slice(half * sublanes, (half + 1) * sublanes)
+                        index = low[span, here]
+                        block = which[span, here]
+                        picked = [jnp.zeros((sublanes, lanes), jnp.float32) for _ in range(count)]
+                        for k in range(columns // lanes):
+                            hit = block == k
+                            for n in range(count):
+                                found = jnp.take_along_axis(
+                                    source[n, span, k * lanes:(k + 1) * lanes], index, axis=1,
+                                    mode="promise_in_bounds",
+                                )
+                                picked[n] = jnp.where(hit, found, picked[n])
+                        total = picked[0] * scaled[0, :, here]
+                        for n in range(1, count):
+                            total = total + picked[n] * scaled[n, :, here]
+                        panels[r, span, here] += total
+
+    walkers(0, 1, 4)
+    batch = source.shape[0]
+
+    @pl.loop(0, (blk_count - 1) // batch)
+    def _(g):
+        first = 1 + g * batch
+        for n in range(batch):
+            for c in range(chunks):
+                far_copy(c, first + n).wait_recv()
+        walkers(first, batch, 2)
 
     @pl.loop(0, chunks)
     def _(c):
@@ -223,18 +238,21 @@
     share = blk_count * rows_own
     rows = near * share
     chunks = columns // (column_block * chunk_blocks)
+    batch = max(n for n in (1, 2, 3) if (blk_count - 1) % n == 0)
     coarse = -(-(columns // column_block) // sublanes) * sublanes
     p = np.arange(rows)
     inner, blk_part, near_part = p % rows_own, p // rows_own % blk_count, p // share
     window = jnp.asarray(((blk_part * near + near_part) * rows_own + inner)[:, None], jnp.int32)
     vmem = pl.BlockSpec(memory_space=pltpu.VMEM)
-    delta = pl.pallas_call(
+    return pl.pallas_call(
         kernel,
         out_shape=jax.ShapeDtypeStruct(g4_old.shape, jnp.float32),
-        in_specs=[pl.BlockSpec(memory_space=pltpu.SMEM), pl.BlockSpec(memory_space=pl.ANY), vmem, vmem, vmem],
+        in_specs=[pl.BlockSpec(memory_space=pltpu.SMEM), pl.BlockSpec(memory_space=pl.ANY), vmem, vmem]
+        + [pl.BlockSpec(memory_space=pl.ANY)] * 2,
         out_specs=vmem,
         scratch_shapes=[
             pltpu.VMEM((own_rows, depth), jnp.bfloat16),
+            pltpu.VMEM(g4_old.shape, jnp.float32),
             pltpu.VMEM((transfers, columns), jnp.int32),
             pltpu.VMEM((transfers, columns), jnp.int32),
             pltpu.VMEM((lanes // sublanes, depth), jnp.float32),
@@ -248,8 +266,10 @@
             pltpu.VMEM((near - 1, share, columns), jnp.float32),
             pltpu.VMEM((blk_count, share, columns), jnp.bfloat16),
             pltpu.VMEM((share, columns), jnp.float32),
-            pltpu.VMEM((transfers, columns), jnp.float32),
-            pltpu.VMEM((sublanes, columns), jnp.float32),
+            pltpu.VMEM((batch, transfers, columns), jnp.float32),
+            pltpu.VMEM((batch, sublanes, columns), jnp.float32),
+            pltpu.SemaphoreType.DMA,
+            pltpu.SemaphoreType.DMA,
             pltpu.SemaphoreType.DMA,
             pltpu.SemaphoreType.DMA((chunks, near - 1)),
             pltpu.SemaphoreType.DMA((chunks, near - 1)),
@@ -258,8 +278,7 @@
         ],
         compiler_params=pltpu.CompilerParams(collective_id=0, has_side_effects=True),
         name="panels",
-    )(weights, walker_mats, vertex, window, transfer_table)
-    return g4_old + delta
+    )(weights, walker_mats, vertex, window, transfer_table, g4_old)
 
 
 def solution(mesh):

time: 25.7 us -> 22.1 us (0.86)
  Pallas kernels: 23.9 us -> 20.3 us
  other arithmetic: 1.6 us -> 0 us
  local copies, waits for them, and re-layouts: 0.01 us -> 1.59 us
    pallas_call x1, Pallas kernels: 23.9 us -> 20.3 us  [local(): pl.pallas_call(kernel, out_shape=jax.ShapeDtypeStruct(g4_old.shape, jnp.f...]
    add x1 -> x0, other arithmetic: 1.6 us -> none  [local(): return g4_old + delta]
    unnamed x2 -> x1, local copies, waits for them, and re-layouts: 0.01 us -> 1.59 us
where the time goes in v2:
time: 22.1 us; the launch traced here: 21.9 us
  Pallas kernels  20.3 us (92%)
  local copies, waits for them, and re-layouts  1.59 us (7%)
    pallas_call x1, Pallas kernels, local(): pl.pallas_call(kernel, out_shape=jax.ShapeDtypeStruct(g4_old.shape, jnp.f...  20.3 us
    unnamed x1, local copies, waits for them, and re-layouts  1.59 us

profile of v2, /device:TPU:0, one launch (start us, length us, event | category | flops | bytes accessed | tf_op | source)
XLA Modules:
  0.0 21.9 jit_solution(6408737360874703362)
XLA Ops:
  0.0 20.3 %panels.1 = f32[1,16,2560]{2,1,0:T(8,128)} custom-call(f32[4]{0:T(128)} %weights.1, bf16[1,1024,2048]{2,1,0:T(8,128)(2,1)} %mats.1, s32[1,2048]{1,0:T(1,128)} %vertex.1, s32[16,1]{1,0:T(8,128)} %constant.2.clone.window, s32[16,2560]{1,0:T(8,128)} %table.1, f32[1,16,2560]{2,1,0:T(8,128)} %old.1), custom_call_target="tpu_custom_call" | custom-call | tf_op jit(solution)/shard_map/panels/pallas_call | solution.py:247
  20.3 1.6 %copy.8 = f32[1,16,2560]{2,1,0:T(8,128)} copy(f32[1,16,2560]{2,1,0:T(8,128)} %panels.1) | data formatting | bytes 327680

commit v3 on v2

--- a/solution.py
+++ b/solution.py
@@ -211,15 +211,14 @@
                         panels[r, span, here] += total
 
     walkers(0, 1, 4)
-    batch = source.shape[0]
-
-    @pl.loop(0, (blk_count - 1) // batch)
-    def _(g):
-        first = 1 + g * batch
-        for n in range(batch):
-            for c in range(chunks):
-                far_copy(c, first + n).wait_recv()
-        walkers(first, batch, 2)
+
+    @pl.loop(0, blk_count - 1)
+    def _(i):
+        origin = i + (i + blk_count - b) // blk_count
+        d = lax.rem(b + blk_count - origin, blk_count)
+        for c in range(chunks):
+            far_copy(c, d).wait_recv()
+        walkers(d, 1, 4)
 
     @pl.loop(0, chunks)
     def _(c):
@@ -238,7 +237,6 @@
     share = blk_count * rows_own
     rows = near * share
     chunks = columns // (column_block * chunk_blocks)
-    batch = max(n for n in (1, 2, 3) if (blk_count - 1) % n == 0)
     coarse = -(-(columns // column_block) // sublanes) * sublanes
     p = np.arange(rows)
     inner, blk_part, near_part = p % rows_own, p // rows_own % blk_count, p // share
@@ -246,7 +244,7 @@
     vmem = pl.BlockSpec(memory_space=pltpu.VMEM)
     return pl.pallas_call(
         kernel,
-        out_shape=jax.ShapeDtypeStruct(g4_old.shape, jnp.float32),
+        out_shape=pltpu.VMEM(g4_old.shape, jnp.float32),
         in_specs=[pl.BlockSpec(memory_space=pltpu.SMEM), pl.BlockSpec(memory_space=pl.ANY), vmem, vmem]
         + [pl.BlockSpec(memory_space=pl.ANY)] * 2,
         out_specs=vmem,
@@ -266,8 +264,8 @@
             pltpu.VMEM((near - 1, share, columns), jnp.float32),
             pltpu.VMEM((blk_count, share, columns), jnp.bfloat16),
             pltpu.VMEM((share, columns), jnp.float32),
-            pltpu.VMEM((batch, transfers, columns), jnp.float32),
-            pltpu.VMEM((batch, sublanes, columns), jnp.float32),
+            pltpu.VMEM((1, transfers, columns), jnp.float32),
+            pltpu.VMEM((1, sublanes, columns), jnp.float32),
             pltpu.SemaphoreType.DMA,
             pltpu.SemaphoreType.DMA,
             pltpu.SemaphoreType.DMA,

time: 22.1 us -> 20 us (0.905)
  Pallas kernels: 20.3 us -> 19.1 us
  local copies, waits for them, and re-layouts: 1.59 us -> 0.67 us
    pallas_call x1, Pallas kernels: 20.3 us -> 19.1 us  [local(): pl.pallas_call(kernel, out_shape=pltpu.VMEM(g4_old.shape, jnp.float32), i...]
    unnamed x1, local copies, waits for them, and re-layouts: 1.59 us -> 0.67 us
where the time goes in v3:
time: 20 us; the launch traced here: 19.8 us
  Pallas kernels  19.1 us (96%)
  local copies, waits for them, and re-layouts  0.67 us (3%)
    pallas_call x1, Pallas kernels, local(): pl.pallas_call(kernel, out_shape=pltpu.VMEM(g4_old.shape, jnp.float32), i...  19.1 us
    unnamed x1, local copies, waits for them, and re-layouts  0.67 us

profile of v3, /device:TPU:0, one launch (start us, length us, event | category | flops | bytes accessed | tf_op | source)
XLA Modules:
  0.0 19.8 jit_solution(11428233076475027253)
XLA Ops:
  0.0 19.1 %panels.1 = f32[1,16,2560]{2,1,0:T(8,128)S(1)} custom-call(f32[4]{0:T(128)} %weights.1, bf16[1,1024,2048]{2,1,0:T(8,128)(2,1)} %mats.1, s32[1,2048]{1,0:T(1,128)} %vertex.1, s32[16,1]{1,0:T(8,128)} %constant.2.clone.window, s32[16,2560]{1,0:T(8,128)} %table.1, f32[1,16,2560]{2,1,0:T(8,128)} %old.1), custom_call_target="tpu_custom_call" | custom-call | tf_op jit(solution)/shard_map/panels/pallas_call | solution.py:245
  19.1 0.7 %copy.8 = f32[1,16,2560]{2,1,0:T(8,128)} copy(f32[1,16,2560]{2,1,0:T(8,128)S(1)} %panels.1) | data formatting | bytes 327680

commit v4 on v3

--- a/solution.py
+++ b/solution.py
@@ -113,13 +113,13 @@
     turn_sin[...] = sin
     cos, sin = phases(row_of(sublanes) * 2 + 1, verts)
 
+    fetch.wait()
+    inner = jnp.dot(left, slab[...], preferred_element_type=jnp.float32)
     for h in range(steps):
         ch, sh = turn_cos[h:h + 1, :], turn_sin[h:h + 1, :]
         fine_cos[h * sublanes:(h + 1) * sublanes, :] = ch * cos - sh * sin
         fine_sin[h * sublanes:(h + 1) * sublanes, :] = sh * cos + ch * sin
 
-    fetch.wait()
-    inner = jnp.dot(left, slab[...], preferred_element_type=jnp.float32)
     high = inner.astype(jnp.bfloat16)
     pair[0:rows, :] = high
     pair[rows:2 * rows, :] = (inner - high.astype(jnp.float32)).astype(jnp.bfloat16)
@@ -133,16 +133,19 @@
             block = c * chunk_blocks + part
             a_plus = coarse_plus[pl.ds(block, 1), :]
             a_minus = coarse_minus[pl.ds(block, 1), :]
-            below, above = [], []
-            for g in range(lanes // 16):
-                p = a_plus * fine_cos[g * 16:(g + 1) * 16, :]
-                q = a_minus * fine_sin[g * 16:(g + 1) * 16, :]
-                below.append((p - q).astype(jnp.bfloat16))
-                above.append((p + q).astype(jnp.bfloat16))
-            both = lax.dot_general(
-                pair[...], jnp.concatenate(below + above, axis=0), (((1,), (1,)), ((), ())),
-                preferred_element_type=jnp.float32,
-            )
+            both = jnp.zeros((2 * rows, column_block), jnp.float32)
+            for k in range(depth // 256):
+                tile = slice(k * 256, (k + 1) * 256)
+                below, above = [], []
+                for g in range(lanes // 16):
+                    p = a_plus[:, tile] * fine_cos[g * 16:(g + 1) * 16, tile]
+                    q = a_minus[:, tile] * fine_sin[g * 16:(g + 1) * 16, tile]
+                    below.append((p - q).astype(jnp.bfloat16))
+                    above.append((p + q).astype(jnp.bfloat16))
+                both = both + lax.dot_general(
+                    pair[:, tile], jnp.concatenate(below + above, axis=0), (((1,), (1,)), ((), ())),
+                    preferred_element_type=jnp.float32,
+                )
             total = both[0:rows] + both[rows:2 * rows]
             here = pl.ds(pl.multiple_of(block * column_block, column_block), column_block)
             for q in range(near):

time: 20 us -> 20 us (level)
  no operation moved by 1% of the time
where the time goes in v4:
time: 20 us; the launch traced here: 19.8 us
  Pallas kernels  19.1 us (96%)
  local copies, waits for them, and re-layouts  0.67 us (3%)
    pallas_call x1, Pallas kernels, local(): pl.pallas_call(kernel, out_shape=pltpu.VMEM(g4_old.shape, jnp.float32), i...  19.1 us
    unnamed x1, local copies, waits for them, and re-layouts  0.67 us

profile of v4, /device:TPU:0, one launch (start us, length us, event | category | flops | bytes accessed | tf_op | source)
XLA Modules:
  0.0 19.8 jit_solution(14606806209629254346)
XLA Ops:
  0.0 19.1 %panels.1 = f32[1,16,2560]{2,1,0:T(8,128)S(1)} custom-call(f32[4]{0:T(128)} %weights.1, bf16[1,1024,2048]{2,1,0:T(8,128)(2,1)} %mats.1, s32[1,2048]{1,0:T(1,128)} %vertex.1, s32[16,1]{1,0:T(8,128)} %constant.2.clone.window, s32[16,2560]{1,0:T(8,128)} %table.1, f32[1,16,2560]{2,1,0:T(8,128)} %old.1), custom_call_target="tpu_custom_call" | custom-call | tf_op jit(solution)/shard_map/panels/pallas_call | solution.py:248
  19.1 0.7 %copy.8 = f32[1,16,2560]{2,1,0:T(8,128)} copy(f32[1,16,2560]{2,1,0:T(8,128)S(1)} %panels.1) | data formatting | bytes 327680
